TPU v7x, 32 devices: a whole 2x2x4 slice. The times are simulated.
32 devices in a mesh: fsdp: 8 (over y, x, core), ctx: 4 (over z).
Axes of the slice: x: 2, y: 2, z: 4, core: 2. Of those that a mesh axis runs over, the one named last changes fastest.
Arguments:
- tokens: bfloat16 [4096, 8192], P('fsdp'), may hold values from -12 to 12
- wq: bfloat16 [8192, 4096], P('fsdp', 'ctx'), may hold values from -0.0625 to 0.0625
- wo: bfloat16 [4096, 8192], P('ctx', 'fsdp'), may hold values from -1.5 to 1.5
- key_cache: bfloat16 [8192, 1024], P(('fsdp', 'ctx')), may hold values from -500 to 500, as said below
- value_cache: bfloat16 [8192, 1024], P(('fsdp', 'ctx')), may hold values from -6 to 6
- key_blocks: int32 [8, 4, 8], P('fsdp'), may hold values from 0 to 7, as said below
Outputs:
- mixed: bfloat16 [4096, 8192], P('fsdp', 'ctx')
Inputs may be any that keep to these rules, and one draw needn't show every extreme that they name: `key_cache`: keys of order one; a sequence's first block may hold much larger ones. `key_blocks`: for query block b of sequence s, entries 0 to 2 name key blocks 8 - 4 + b - 2, 4 + b - 1 and 4 + b; entries 3 and 4 name blocks 0 and 1; the last 3 entries are random blocks. Counting the random entries of a sequence over its query blocks in order as t = 0, 1, ..., the t-th lies in blocks k * 2 to (k+1) * 2 - 1 with k = 1 + t mod (2); entries may repeat.
All inputs are finite; a program needn't handle non-finite values.
Results may differ from a plain program's by a relative error of at most 0.018.
Values may be sent and summed in bfloat16 or wider, within the bound.
A program may use at most 128 MiB of HBM per device.

v0:
```python
import functools

import jax
import jax.numpy as jnp
from jax import lax
from jax.experimental import pallas as pl
from jax.experimental.pallas import tpu as pltpu
from jax.sharding import PartitionSpec as P

HEAD = 128
BLOCK = 128
LANES = 128
AHEAD = 4
MESH = pl.DeviceIdType.MESH

rope_base = 1000000.0


def tables(row_count, key_total):
    half_width = HEAD // 2
    frequency = rope_base ** (-(jnp.arange(half_width, dtype=jnp.float32) * 2.0) / HEAD)
    positions = key_total - row_count + jnp.arange(row_count, dtype=jnp.int32)
    angles = positions.astype(jnp.float32)[:, None] * frequency[None, :]
    cosine = jnp.cos(angles) * HEAD ** (-0.5)
    sine = jnp.sin(angles) * HEAD ** (-0.5)
    return jnp.concatenate([cosine, cosine], axis=1), jnp.concatenate([-sine, sine], axis=1)


def low_bit(m):
    return m & -m


def high_bit(m):
    return 1 << (m.bit_length() - 1)


def route(mask, piece):
    return low_bit(mask) if piece % 2 == 0 else high_bit(mask)


def kernel(
    cfg,
    lists, tokens, wq, wo, kc, vc, cos_ref, sin_ref,
    out,
    tok, wq_buf, wo_buf, k_buf, v_buf, acc, qc, k_pick, v_pick, bias, ctx_all, ctx_perm, staged, hop,
    tok_sem, own_sem, send_sem, wq_sem, wo_sem, kv_send, kv_sem, ctx_send, ctx_sem,
    move_send, move_sem, keep_sem, hop_send, hop_sem, out_sem,
):
    n_f, n_c, nq, nw = cfg
    chips = n_f // 2
    bits = [1 << i for i in range(chips.bit_length() - 1)]
    masks = sorted(range(1, chips), key=lambda m: (bin(m).count("1"), m))
    f = lax.axis_index("fsdp")
    c = lax.axis_index("ctx")
    rows = tok.shape[1]
    depth = tok.shape[2]
    qcols = wq_buf.shape[2]
    qp = wq_buf.shape[1] // nq
    wo_cols = wo.shape[1]
    wp = wo_buf.shape[2] // nw
    part = wo.shape[0] // chips
    ratio = n_f // n_c
    blk_dev = kc.shape[0]
    kv_cols = k_buf.shape[2]
    kv_local = kv_cols // HEAD
    group = qcols // kv_cols
    n_blocks = k_buf.shape[0]
    q_blocks = rows // BLOCK
    n_list = lists.shape[2]

    def flip(x):
        bit, total = 1, 0
        while bit < n_f:
            total += lax.rem(lax.div(f, bit) + x // bit, 2) * bit
            bit *= 2
        return total

    def peer(x):
        return (flip(x), c)

    barrier = pltpu.get_barrier_semaphore()
    me = f * n_c + c

    @pl.loop(1, n_f * n_c)
    def _(d):
        other = lax.rem(me + d, n_f * n_c)
        pl.semaphore_signal(
            barrier, inc=1, device_id=(lax.div(other, n_c), lax.rem(other, n_c)), device_id_type=MESH
        )

    pl.semaphore_wait(barrier, n_f * n_c - 1)

    sent = []

    def view(kind, ref, s):
        if kind == 0:
            return ref.at[pl.ds(s * qp, qp), :]
        return ref.at[:, pl.ds(s * wp, wp)]

    shard = (wq, wo_buf.at[0])
    bufs = (wq_buf, wo_buf)
    sems = (wq_sem, wo_sem)
    counts = (nq, nw)

    def send(kind, src, slot, s, to):
        copy = pltpu.make_async_remote_copy(
            src_ref=src,
            dst_ref=view(kind, bufs[kind].at[slot], s),
            send_sem=send_sem.at[len(sent)],
            recv_sem=sems[kind].at[slot, s],
            device_id=peer(to),
            device_id_type=MESH,
        )
        copy.start()
        sent.append(copy)

    def arrived(kind, slot, s):
        pltpu.make_async_remote_copy(
            src_ref=view(kind, bufs[kind].at[slot], s),
            dst_ref=view(kind, bufs[kind].at[slot], s),
            send_sem=send_sem.at[0],
            recv_sem=sems[kind].at[slot, s],
            device_id=peer(1),
            device_id_type=MESH,
        ).wait_recv()

    stream = [(0, s) for s in range(nq)] + [(1, s) for s in range(nw)]

    def directs(i):
        if i < len(stream):
            kind, s = stream[i]
            for b in bits:
                send(kind, view(kind, shard[kind], s), 2 * b, s, 2 * b)

    def kv_copy(which, d):
        other = lax.rem(c + d, n_c)
        src, dst = ((kc, k_buf), (vc, v_buf))[which]
        return pltpu.make_async_remote_copy(
            src_ref=src.at[:, :, pl.ds(pl.multiple_of(other * kv_cols, LANES), kv_cols)],
            dst_ref=dst.at[pl.ds(c * blk_dev, blk_dev)],
            send_sem=kv_send.at[which, d],
            recv_sem=kv_sem.at[which, d],
            device_id=(f, other),
            device_id_type=MESH,
        )

    core = lax.rem(f, 2)
    chip = lax.div(f, 2)

    def piece(q):
        return wo.at[pl.ds(pl.multiple_of(q * part, part), part), :]

    def hop_copy(q, source):
        return pltpu.make_async_remote_copy(
            src_ref=piece(q),
            dst_ref=hop.at[source],
            send_sem=hop_send.at[q],
            recv_sem=hop_sem.at[source],
            device_id=(q * 2 + core, c),
            device_id_type=MESH,
        )

    def move_dst(i, plane):
        return wo_buf.at[
            0,
            pl.ds(pl.multiple_of(plane * part, part), part),
            pl.ds(pl.multiple_of(i * wo_cols, wo_cols), wo_cols),
        ]

    def owner(p):
        source = p * 2 + core
        return lax.div(source, ratio), lax.div(lax.rem(source, ratio), 2)

    def move(src, p):
        home, i = owner(p)
        return pltpu.make_async_remote_copy(
            src_ref=src,
            dst_ref=move_dst(i, c),
            send_sem=move_send.at[p],
            recv_sem=move_sem.at[i, c],
            device_id=(f, home),
            device_id_type=MESH,
        )

    def keep(src, p):
        _, i = owner(p)
        return pltpu.make_async_copy(src, move_dst(i, c), keep_sem.at[i])

    def start_hops():
        @pl.loop(1, chips)
        def _(d):
            hop_copy(lax.rem(chip + d, chips), chip).start()

    def forward(src, p):
        home, _ = owner(p)

        @pl.when(home == c)
        def _():
            keep(src, p).start()

        @pl.when(home != c)
        def _():
            move(src, p).start()

    def start_moves():
        forward(piece(chip), chip)

        @pl.loop(1, chips)
        def _(d):
            p = lax.rem(chip + d, chips)
            hop_copy(p, p).wait_recv()
            forward(hop.at[p], p)

    def wait_moves():
        for i in range(ratio // 2):
            keep(piece(chip), lax.div(c * ratio + 2 * i, 2)).wait()

            @pl.loop(1, n_c)
            def _(d):
                plane = lax.rem(c + d, n_c)
                pltpu.make_async_remote_copy(
                    src_ref=move_dst(i, plane),
                    dst_ref=move_dst(i, plane),
                    send_sem=move_send.at[0],
                    recv_sem=move_sem.at[i, plane],
                    device_id=peer(1),
                    device_id_type=MESH,
                ).wait_recv()

    start_hops()
    directs(0)
    for s in range(nq):
        send(0, view(0, wq, s), 1, s, 1)
    directs(1)

    def tok_copy(j):
        start = pl.multiple_of(flip(j) * depth, LANES)
        return pltpu.make_async_copy(tokens.at[:, pl.ds(start, depth)], tok.at[j], tok_sem.at[j])

    own_q = pltpu.make_async_copy(wq, wq_buf.at[0], own_sem.at[0])
    own_q.start()
    for j in range(n_f):
        tok_copy(j).start()
    kv_sent = []
    for d in range(1, n_c):
        for which in range(2):
            copy = kv_copy(which, d)
            copy.start()
            kv_sent.append(copy)
    mine = pl.ds(pl.multiple_of(c * kv_cols, LANES), kv_cols)
    own_k = pltpu.make_async_copy(kc.at[:, :, mine], k_buf.at[pl.ds(c * blk_dev, blk_dev)], own_sem.at[2])
    own_v = pltpu.make_async_copy(vc.at[:, :, mine], v_buf.at[pl.ds(c * blk_dev, blk_dev)], own_sem.at[3])
    own_k.start()
    own_v.start()

    acc[...] = jnp.zeros_like(acc)
    tile = min(256, qcols)
    tiles = qcols // tile

    def q_piece(j, s):
        left = tok[j, :, s * qp:(s + 1) * qp]

        @pl.loop(0, tiles)
        def _(t):
            cols = pl.ds(pl.multiple_of(t * tile, tile), tile)
            acc[:, cols] += jnp.dot(
                left, wq_buf[j, s * qp:(s + 1) * qp, cols], preferred_element_type=jnp.float32
            )

    def q_whole(j):
        @pl.loop(0, tiles)
        def _(t):
            cols = pl.ds(pl.multiple_of(t * tile, tile), tile)
            acc[:, cols] += jnp.dot(tok[j], wq_buf[j, :, cols], preferred_element_type=jnp.float32)

    own_q.wait()
    for j in range(n_f):
        tok_copy(j).wait()
    for s in range(nq):
        arrived(0, 1, s)

    @pl.loop(0, 2)
    def _(j):
        q_whole(j)

    def pass_on(i):
        kind, s = stream[i]
        for m in masks:
            arrived(kind, 2 * m, s)
            piece = view(kind, bufs[kind].at[2 * m], s)
            for b in bits:
                if not (m & b) and route(m | b, s) == b:
                    send(kind, piece, 2 * (m | b), s, 2 * b)
            send(kind, piece, 2 * m + 1, s, 1)
            if m == bits[-1] and kind == 0 and i + 2 < nq:
                directs(i + 2)
            if m == bits[-1] and kind == 1:
                directs(i + AHEAD)

    for s in range(nq):
        pass_on(s)
        if s == 0:
            start_moves()
        if s == max(0, nq - 2):
            wait_moves()
            directs(nq)
            for i in range(nw):
                send(1, view(1, shard[1], i), 1, i, 1)
        if s == nq - 1:
            for i in range(1, AHEAD):
                directs(nq + i)

        @pl.loop(2, n_f)
        def _(j):
            @pl.when(lax.rem(j, 2) == 1)
            def _():
                arrived(0, j, s)

            q_piece(j, s)

    for h in range(qcols // HEAD):
        cols = slice(h * HEAD, (h + 1) * HEAD)
        x = acc[:, cols]
        turned = x * cos_ref[...] + pltpu.roll(x, HEAD // 2, 1) * sin_ref[...]
        qc[:, cols] = turned.astype(jnp.bfloat16)

    own_k.wait()
    own_v.wait()
    for copy in kv_sent:
        copy.wait_recv()

    def ctx_copy(b, d):
        q_rows = pl.ds(pl.multiple_of(b * BLOCK, BLOCK), BLOCK)
        return pltpu.make_async_remote_copy(
            src_ref=qc.at[q_rows],
            dst_ref=ctx_all.at[c, q_rows],
            send_sem=ctx_send.at[b, d],
            recv_sem=ctx_sem.at[b, d],
            device_id=(f, lax.rem(c + d, n_c)),
            device_id_type=MESH,
        )

    @pl.loop(0, q_blocks)
    def _(b):
        q_rows = pl.ds(pl.multiple_of(b * BLOCK, BLOCK), BLOCK)
        own_block = n_blocks - q_blocks + b
        later = lax.broadcasted_iota(jnp.int32, (BLOCK, BLOCK), 1) > lax.broadcasted_iota(
            jnp.int32, (BLOCK, BLOCK), 0
        )
        for n in range(n_list):
            entry = lists[0, b, n]
            hide = jnp.where(entry == own_block, -jnp.inf, 0.0)
            bias[:, n * BLOCK:(n + 1) * BLOCK] = jnp.where(later, hide, 0.0)
        for g in range(kv_local):
            head_cols = slice(g * HEAD, (g + 1) * HEAD)
            for n in range(n_list):
                entry = lists[0, b, n]
                k_pick[n * BLOCK:(n + 1) * BLOCK, :] = k_buf[entry, :, head_cols]
                v_pick[n * BLOCK:(n + 1) * BLOCK, :] = v_buf[entry, :, head_cols]
            for i in range(group):
                h = g * group + i
                cols = slice(h * HEAD, (h + 1) * HEAD)
                scores = lax.dot_general(
                    qc[q_rows, cols], k_pick[...], (((1,), (1,)), ((), ())),
                    preferred_element_type=jnp.float32,
                ) + bias[...]
                top = jnp.max(scores, axis=1, keepdims=True)
                raised = jnp.exp(scores - top)
                total = jnp.sum(raised, axis=1, keepdims=True)
                mixed = jnp.dot(
                    raised.astype(jnp.bfloat16), v_pick[...], preferred_element_type=jnp.float32
                )
                qc[q_rows, cols] = (mixed / total).astype(jnp.bfloat16)

        @pl.loop(1, n_c)
        def _(d):
            ctx_copy(b, d).start()

    acc[...] = jnp.zeros_like(acc)

    def share(j, s):
        target = flip(j)
        i, offset = divmod(s * wp, wo_cols)
        start = pl.multiple_of((2 * i + lax.rem(target, 2)) * wo_cols + offset, LANES)
        acc[:, pl.ds(start, wp)] += jnp.dot(
            ctx_perm[lax.div(target, 2)], wo_buf[j, :, s * wp:(s + 1) * wp],
            preferred_element_type=jnp.float32,
        )

    def out_copy(s, k):
        i, offset = divmod(s * wp, wo_cols)
        cols = pl.ds((2 * i + k) * wo_cols + offset, wp)
        return pltpu.make_async_copy(staged.at[:, cols], out.at[:, cols], out_sem.at[s, k])

    for s in range(nw):
        pass_on(nq + s)
    ctx_all[c] = qc[...]

    @pl.loop(0, q_blocks)
    def _(b):
        @pl.loop(1, n_c)
        def _(d):
            ctx_copy(b, d).wait_recv()

    for q in range(chips):
        for plane in range(n_c):
            ctx_perm[q, :, plane * part:(plane + 1) * part] = ctx_all[
                plane, :, q * part:(q + 1) * part
            ]
    for s in range(nw):
        @pl.loop(0, n_f)
        def _(j):
            @pl.when(lax.rem(j, 2) == 1)
            def _():
                arrived(1, j, s)

            share(j, s)

        for k in range(2):
            i, offset = divmod(s * wp, wo_cols)
            cols = pl.ds((2 * i + k) * wo_cols + offset, wp)
            staged[:, cols] = acc[:, cols].astype(jnp.bfloat16)
            out_copy(s, k).start()

    assert len(sent) == send_sem.shape[0]
    for copy in sent + kv_sent:
        copy.wait_send()

    @pl.loop(0, q_blocks)
    def _(b):
        @pl.loop(1, n_c)
        def _(d):
            ctx_copy(b, d).wait_send()

    @pl.loop(0, chips)
    def _(q):
        @pl.when(q != chip)
        def _():
            hop_copy(q, chip).wait_send()

        home, _ = owner(q)

        @pl.when(home != c)
        def _():
            move(piece(chip), q).wait_send()

    for s in range(nw):
        for k in range(2):
            out_copy(s, k).wait()


def body(n_f, n_c, tokens, wq, wo, key_cache, value_cache, key_blocks):
    rows, width = tokens.shape
    depth = width // n_f
    qcols = wq.shape[1]
    cache = key_cache.shape[0]
    blk_dev = cache // BLOCK
    kv_cols = key_cache.shape[1] // n_c
    n_list = key_blocks.shape[2]
    cosine, sine = tables(rows, cache * n_c)
    nq = max(1, min(4, wq.shape[0] // LANES))
    ratio = n_f // n_c
    chips = n_f // 2
    part = wo.shape[0] // chips
    moved = (part * n_c, wo.shape[1] * ratio // 2)
    nw = max(1, min(4, moved[1] // LANES))
    any_spec = pl.BlockSpec(memory_space=pl.ANY)
    vmem_spec = pl.BlockSpec(memory_space=pltpu.VMEM)
    bf16 = jnp.bfloat16
    dma = pltpu.SemaphoreType.DMA
    return pl.pallas_call(
        functools.partial(kernel, (n_f, n_c, nq, nw)),
        out_shape=jax.ShapeDtypeStruct((rows, width // n_c), bf16),
        in_specs=[pl.BlockSpec(memory_space=pltpu.SMEM)] + [any_spec] * 5 + [vmem_spec] * 2,
        out_specs=any_spec,
        scratch_shapes=[
            pltpu.VMEM((n_f, rows, depth), bf16),
            pltpu.VMEM((n_f,) + wq.shape, bf16),
            pltpu.VMEM((n_f,) + moved, bf16),
            pltpu.VMEM((blk_dev * n_c, BLOCK, kv_cols), bf16),
            pltpu.VMEM((blk_dev * n_c, BLOCK, kv_cols), bf16),
            pltpu.VMEM((rows, max(qcols, width // n_c)), jnp.float32),
            pltpu.VMEM((rows, qcols), bf16),
            pltpu.VMEM((n_list * BLOCK, HEAD), bf16),
            pltpu.VMEM((n_list * BLOCK, HEAD), bf16),
            pltpu.VMEM((BLOCK, n_list * BLOCK), jnp.float32),
            pltpu.VMEM((n_c, rows, qcols), bf16),
            pltpu.VMEM((chips, rows, n_c * part), bf16),
            pltpu.VMEM((rows, width // n_c), bf16),
            pltpu.VMEM((chips, part, wo.shape[1]), bf16),
            dma((n_f,)),
            dma((4,)),
            dma(((nq + nw) * (n_f - 1),)),
            dma((n_f, nq)),
            dma((n_f, nw)),
            dma((2, n_c)),
            dma((2, n_c)),
            dma((rows // BLOCK, n_c)),
            dma((rows // BLOCK, n_c)),
            dma((chips,)),
            dma((ratio // 2, n_c)),
            dma((ratio // 2,)),
            dma((chips,)),
            dma((chips,)),
            dma((nw, 2)),
        ],
        compiler_params=pltpu.CompilerParams(
            collective_id=0, has_side_effects=True, vmem_limit_bytes=67043328
        ),
    )(
        key_blocks,
        tokens,
        wq,
        wo,
        key_cache.reshape(blk_dev, BLOCK, key_cache.shape[1]),
        value_cache.reshape(blk_dev, BLOCK, value_cache.shape[1]),
        cosine,
        sine,
    )


def solution(mesh):
    in_specs = (
        P("fsdp", None),
        P("fsdp", "ctx"),
        P("ctx", "fsdp"),
        P(("fsdp", "ctx"), None),
        P(("fsdp", "ctx"), None),
        P("fsdp", None, None),
    )
    step = functools.partial(body, mesh.shape["fsdp"], mesh.shape["ctx"])
    return jax.shard_map(
        step, mesh=mesh, in_specs=in_specs, out_specs=P("fsdp", "ctx"), check_vma=False
    )
```

profile of v0, /device:TPU:29, one launch (start us, length us, event | category | flops | bytes accessed | tf_op | source)
XLA Modules:
  0.0 251.7 jit_solution(15889141022149336288)
XLA Ops:
  0.0 1.0 fusion.2
  1.0 1.0 pad_maximum_fusion
  2.1 246.4 %shard_map.64 = bf16[512,2048]{1,0:T(8,128)(2,1)} custom-call(s32[1,4,8]{2,1,0:T(4,128)} %lists.1, bf16[512,8192]{1,0:T(8,128)(2,1)} %tokens.1, bf16[1024,1024]{1,0:T(8,128)(2,1)} %wq.1, bf16[1024,1024]{1,0:T(8,128)(2,1)} %wo.1, bf16[2,128,1024]{2,1,0:T(8,128)(2,1)} %bitcast.2, bf16[2,128,1024]{2,1,0:T(8,128)(2,1)} %bitcast.3, ...), custom_call_target="tpu_custom_call" | custom-call | tf_op jit(solution)/shard_map/pallas_call | solution.py:471
  248.5 3.2 %copy.8 = bf16[512,2048]{1,0:T(8,128)(2,1)} copy(bf16[512,2048]{1,0:T(8,128)(2,1)} %shard_map.64) | data formatting | bytes 4194304
  (2 shorter events, 0.0 us)
where the time goes:
time: 252 us
  Pallas kernels  246 us (98%)
  local copies, waits for them, and re-layouts  3.16 us (1%)
    pallas_call x1, Pallas kernels, body(): pl.pallas_call(functools.partial(kernel, (n_f, n_c, nq, nw)), out_shape=j...  246 us

commit v1 on v0

v1 whole, which is shorter than its diff:
```python
import functools

import jax
import jax.numpy as jnp
import numpy as np
from jax import lax
from jax.experimental import pallas as pl
from jax.experimental.pallas import tpu as pltpu
from jax.sharding import PartitionSpec as P

HEAD = 128
BLOCK = 128
LANES = 128
AHEAD = 2
HALVES = 2
MESH = pl.DeviceIdType.MESH

rope_base = 1000000.0


def tables(row_count, key_total):
    half_width = HEAD // 2
    exponent = -(np.arange(half_width, dtype=np.float32) * np.float32(2.0)) / np.float32(HEAD)
    frequency = np.power(np.float32(rope_base), exponent, dtype=np.float32)
    positions = (key_total - row_count + np.arange(row_count)).astype(np.float32)
    angles = positions[:, None] * frequency[None, :]
    scale = np.float32(HEAD ** (-0.5))
    cosine = np.cos(angles) * scale
    sine = np.sin(angles) * scale
    return np.concatenate([cosine, cosine], axis=1), np.concatenate([-sine, sine], axis=1)


def low_bit(m):
    return m & -m


def high_bit(m):
    return 1 << (m.bit_length() - 1)


def route(mask, half):
    return low_bit(mask) if half % 2 == 0 else high_bit(mask)


def kernel(
    cfg,
    lists, tokens, wq, wo, kc, vc, cos_in, sin_in,
    out,
    tok, wq_buf, wo_buf, k_buf, v_buf, acc, qc, k_pick, v_pick, bias, ctx_all, ctx_perm, staged, hop, cos_ref, sin_ref,
    tok_sem, own_sem, send_sem, wq_sem, wo_sem, kv_send, kv_sem, ctx_send, ctx_sem,
    move_send, move_sem, keep_sem, hop_send, hop_sem, out_sem,
):
    n_f, n_c, nq, nw = cfg
    chips = n_f // 2
    bits = [1 << i for i in range(chips.bit_length() - 1)]
    levels = len(bits)
    masks = sorted(range(1, chips), key=lambda m: (bin(m).count("1"), m))
    level = {m: bin(m).count("1") for m in masks}
    f = lax.axis_index("fsdp")
    c = lax.axis_index("ctx")
    rows = tok.shape[1]
    depth = tok.shape[2]
    qcols = wq_buf.shape[2]
    qp = qcols // nq
    qh = wq_buf.shape[1] // HALVES
    wo_cols = wo.shape[1]
    wp = wo_buf.shape[2] // nw
    wh = wo_buf.shape[1] // HALVES
    part = wo.shape[0] // chips
    ratio = n_f // n_c
    blk_dev = kc.shape[0]
    kv_cols = k_buf.shape[2]
    group = qcols // kv_cols
    n_blocks = k_buf.shape[0]
    q_blocks = rows // BLOCK
    n_list = lists.shape[2]

    def flip(x):
        bit, total = 1, 0
        while bit < n_f:
            total += lax.rem(lax.div(f, bit) + x // bit, 2) * bit
            bit *= 2
        return total

    def peer(x):
        return (flip(x), c)

    sent = []

    def view(kind, ref, s, h):
        if kind == 0:
            return ref.at[pl.ds(h * qh, qh), pl.ds(s * qp, qp)]
        return ref.at[pl.ds(h * wh, wh), pl.ds(s * wp, wp)]

    shard = (wq, wo_buf.at[0])
    bufs = (wq_buf, wo_buf)
    sems = (wq_sem, wo_sem)
    stream = [(0, s) for s in range(nq)] + [(1, s) for s in range(nw)]

    def send(kind, src, slot, s, h, to):
        copy = pltpu.make_async_remote_copy(
            src_ref=src,
            dst_ref=view(kind, bufs[kind].at[slot], s, h),
            send_sem=send_sem.at[len(sent)],
            recv_sem=sems[kind].at[slot, s, h],
            device_id=peer(to),
            device_id_type=MESH,
        )
        copy.start()
        sent.append(copy)

    def arrived(kind, slot, s, h):
        pltpu.make_async_remote_copy(
            src_ref=view(kind, bufs[kind].at[slot], s, h),
            dst_ref=view(kind, bufs[kind].at[slot], s, h),
            send_sem=send_sem.at[0],
            recv_sem=sems[kind].at[slot, s, h],
            device_id=peer(1),
            device_id_type=MESH,
        ).wait_recv()

    def directs(i):
        if i < len(stream):
            kind, s = stream[i]
            for h in range(HALVES):
                for b in bits:
                    send(kind, view(kind, shard[kind], s, h), 2 * b, s, h, 2 * b)

    def to_partner(kind, s):
        for h in range(HALVES):
            send(kind, view(kind, shard[kind], s, h), 1, s, h, 1)

    def pass_level(i, lev):
        if not 0 <= i < len(stream):
            return
        kind, s = stream[i]
        for h in range(HALVES):
            for m in masks:
                if level[m] != lev:
                    continue
                arrived(kind, 2 * m, s, h)
                block = view(kind, bufs[kind].at[2 * m], s, h)
                for b in bits:
                    if not (m & b) and route(m | b, h) == b:
                        send(kind, block, 2 * (m | b), s, h, 2 * b)
                send(kind, block, 2 * m + 1, s, h, 1)

    def kv_copy(which, d):
        other = lax.rem(c + d, n_c)
        src, dst = ((kc, k_buf), (vc, v_buf))[which]
        return pltpu.make_async_remote_copy(
            src_ref=src.at[:, :, pl.ds(pl.multiple_of(other * kv_cols, LANES), kv_cols)],
            dst_ref=dst.at[pl.ds(c * blk_dev, blk_dev)],
            send_sem=kv_send.at[which, d],
            recv_sem=kv_sem.at[which, d],
            device_id=(f, other),
            device_id_type=MESH,
        )

    core = lax.rem(f, 2)
    chip = lax.div(f, 2)

    def piece(q):
        return wo.at[pl.ds(pl.multiple_of(q * part, part), part), :]

    def hop_copy(q, source):
        return pltpu.make_async_remote_copy(
            src_ref=piece(q),
            dst_ref=hop.at[source],
            send_sem=hop_send.at[q],
            recv_sem=hop_sem.at[source],
            device_id=(q * 2 + core, c),
            device_id_type=MESH,
        )

    def move_dst(i, plane):
        return wo_buf.at[
            0,
            pl.ds(pl.multiple_of(plane * part, part), part),
            pl.ds(pl.multiple_of(i * wo_cols, wo_cols), wo_cols),
        ]

    def owner(p):
        source = p * 2 + core
        return lax.div(source, ratio), lax.div(lax.rem(source, ratio), 2)

    def move(src, p):
        home, i = owner(p)
        return pltpu.make_async_remote_copy(
            src_ref=src,
            dst_ref=move_dst(i, c),
            send_sem=move_send.at[p],
            recv_sem=move_sem.at[i, c],
            device_id=(f, home),
            device_id_type=MESH,
        )

    def keep(src, p):
        _, i = owner(p)
        return pltpu.make_async_copy(src, move_dst(i, c), keep_sem.at[i])

    def forward(src, p):
        home, _ = owner(p)

        @pl.when(home == c)
        def _():
            keep(src, p).start()

        @pl.when(home != c)
        def _():
            move(src, p).start()

    def start_moves():
        forward(piece(chip), chip)

        @pl.loop(1, chips)
        def _(d):
            p = lax.rem(chip + d, chips)
            hop_copy(p, p).wait_recv()
            forward(hop.at[p], p)

    def wait_moves():
        for i in range(ratio // 2):
            keep(piece(chip), lax.div(c * ratio + 2 * i, 2)).wait()

            @pl.loop(1, n_c)
            def _(d):
                plane = lax.rem(c + d, n_c)
                pltpu.make_async_remote_copy(
                    src_ref=move_dst(i, plane),
                    dst_ref=move_dst(i, plane),
                    send_sem=move_send.at[0],
                    recv_sem=move_sem.at[i, plane],
                    device_id=peer(1),
                    device_id_type=MESH,
                ).wait_recv()

    def ctx_view(s, origin):
        return ctx_all.at[origin, :, pl.ds(s * qp, qp)]

    def ctx_copy(s, origin, side, src):
        return pltpu.make_async_remote_copy(
            src_ref=src,
            dst_ref=ctx_view(s, origin),
            send_sem=ctx_send.at[s, origin, side],
            recv_sem=ctx_sem.at[s, origin],
            device_id=(f, c + 1 if side else c - 1),
            device_id_type=MESH,
        )

    def ctx_start(s):
        own = qc.at[:, pl.ds(s * qp, qp)]

        @pl.when(c + 1 < n_c)
        def _():
            ctx_copy(s, c, 1, own).start()

        @pl.when(c > 0)
        def _():
            ctx_copy(s, c, 0, own).start()

        ctx_all[c, :, s * qp:(s + 1) * qp] = qc[:, s * qp:(s + 1) * qp]

    def ctx_pass(s, d):
        below = c - d
        above = c + d

        @pl.when(below >= 0)
        def _():
            ctx_copy(s, below, 0, ctx_view(s, below)).wait_recv()

            @pl.when(c + 1 < n_c)
            def _():
                ctx_copy(s, below, 1, ctx_view(s, below)).start()

        @pl.when(above < n_c)
        def _():
            ctx_copy(s, above, 1, ctx_view(s, above)).wait_recv()

            @pl.when(c > 0)
            def _():
                ctx_copy(s, above, 0, ctx_view(s, above)).start()

    def ctx_drain(s):
        @pl.loop(0, n_c)
        def _(origin):
            @pl.when(jnp.logical_and(origin <= c, c + 1 < n_c))
            def _():
                ctx_copy(s, origin, 1, ctx_view(s, origin)).wait_send()

            @pl.when(jnp.logical_and(origin >= c, c > 0))
            def _():
                ctx_copy(s, origin, 0, ctx_view(s, origin)).wait_send()

    tile = min(256, qp)

    def q_part(j, s):
        for t in range(qp // tile):
            cols = slice(s * qp + t * tile, s * qp + (t + 1) * tile)
            acc[:, cols] += jnp.dot(tok[j], wq_buf[j, :, cols], preferred_element_type=jnp.float32)

    def attend(s):
        first = s * qp // HEAD
        heads = range(first, first + qp // HEAD)
        for h in heads:
            cols = slice(h * HEAD, (h + 1) * HEAD)
            x = acc[:, cols]
            turned = x * cos_ref[...] + pltpu.roll(x, HEAD // 2, 1) * sin_ref[...]
            qc[:, cols] = turned.astype(jnp.bfloat16)

        @pl.loop(0, q_blocks)
        def _(b):
            q_rows = pl.ds(pl.multiple_of(b * BLOCK, BLOCK), BLOCK)
            own_block = n_blocks - q_blocks + b
            later = lax.broadcasted_iota(jnp.int32, (BLOCK, BLOCK), 1) > lax.broadcasted_iota(
                jnp.int32, (BLOCK, BLOCK), 0
            )
            for n in range(n_list):
                entry = lists[0, b, n]
                hide = jnp.where(entry == own_block, -jnp.inf, 0.0)
                bias[:, n * BLOCK:(n + 1) * BLOCK] = jnp.where(later, hide, 0.0)
            for g in sorted({h // group for h in heads}):
                head_cols = slice(g * HEAD, (g + 1) * HEAD)
                for n in range(n_list):
                    entry = lists[0, b, n]
                    k_pick[n * BLOCK:(n + 1) * BLOCK, :] = k_buf[entry, :, head_cols]
                    v_pick[n * BLOCK:(n + 1) * BLOCK, :] = v_buf[entry, :, head_cols]
                for h in heads:
                    if h // group != g:
                        continue
                    cols = slice(h * HEAD, (h + 1) * HEAD)
                    scores = lax.dot_general(
                        qc[q_rows, cols], k_pick[...], (((1,), (1,)), ((), ())),
                        preferred_element_type=jnp.float32,
                    ) + bias[...]
                    top = jnp.max(scores, axis=1, keepdims=True)
                    raised = jnp.exp(scores - top)
                    total = jnp.sum(raised, axis=1, keepdims=True)
                    mixed = jnp.dot(
                        raised.astype(jnp.bfloat16), v_pick[...], preferred_element_type=jnp.float32
                    )
                    qc[q_rows, cols] = (mixed / total).astype(jnp.bfloat16)

    def share(j, s):
        target = flip(j)
        i, offset = divmod(s * wp, wo_cols)
        start = pl.multiple_of((2 * i + lax.rem(target, 2)) * wo_cols + offset, LANES)
        acc[:, pl.ds(start, wp)] += jnp.dot(
            ctx_perm[lax.div(target, 2)], wo_buf[j, :, s * wp:(s + 1) * wp],
            preferred_element_type=jnp.float32,
        )

    def out_copy(s, k):
        i, offset = divmod(s * wp, wo_cols)
        cols = pl.ds((2 * i + k) * wo_cols + offset, wp)
        return pltpu.make_async_copy(staged.at[:, cols], out.at[:, cols], out_sem.at[s, k])

    last_slot = 2 * min(m for m in masks if level[m] == levels)

    def shares(s, start, stop):
        @pl.loop(start, stop)
        def _(j):
            @pl.when(lax.rem(j, 2) == 1)
            def _():
                for h in range(HALVES):
                    arrived(1, j, s, h)

            share(j, s)

    def compute_early(i):
        kind, s = stream[i]
        if kind == 1 and levels > 1:
            shares(s, 0, 4)
            if levels == 2:
                shares(s, 4, last_slot)

    def compute(i):
        kind, s = stream[i]
        if kind == 0:
            @pl.loop(2, n_f)
            def _(j):
                @pl.when(lax.rem(j, 2) == 1)
                def _():
                    for h in range(HALVES):
                        arrived(0, j, s, h)

                q_part(j, s)

            attend(s)
            ctx_start(s)
            return
        shares(s, (last_slot if levels == 2 else 4) if levels > 1 else 0, n_f)
        for k in range(2):
            p, offset = divmod(s * wp, wo_cols)
            cols = pl.ds((2 * p + k) * wo_cols + offset, wp)
            staged[:, cols] = acc[:, cols].astype(jnp.bfloat16)
            out_copy(s, k).start()

    def tok_copy(j):
        start = pl.multiple_of(flip(j) * depth, LANES)
        return pltpu.make_async_copy(tokens.at[:, pl.ds(start, depth)], tok.at[j], tok_sem.at[j])

    mine = pl.ds(pl.multiple_of(c * kv_cols, LANES), kv_cols)
    locals_in = [
        pltpu.make_async_copy(wq, wq_buf.at[0], own_sem.at[0]),
        pltpu.make_async_copy(kc.at[:, :, mine], k_buf.at[pl.ds(c * blk_dev, blk_dev)], own_sem.at[1]),
        pltpu.make_async_copy(vc.at[:, :, mine], v_buf.at[pl.ds(c * blk_dev, blk_dev)], own_sem.at[2]),
        pltpu.make_async_copy(cos_in, cos_ref, own_sem.at[3]),
        pltpu.make_async_copy(sin_in, sin_ref, own_sem.at[4]),
    ]

    barrier = pltpu.get_barrier_semaphore()
    signalled = 0
    for x in [1] + [2 * m for m in masks]:
        pl.semaphore_signal(barrier, inc=1, device_id=peer(x), device_id_type=MESH)
        signalled += 1
    for d in range(1, n_c):
        pl.semaphore_signal(barrier, inc=1, device_id=(f, lax.rem(c + d, n_c)), device_id_type=MESH)
        signalled += 1
    for copy in locals_in:
        copy.start()
    for j in range(n_f):
        tok_copy(j).start()
    acc[...] = jnp.zeros_like(acc)
    pl.semaphore_wait(barrier, signalled)

    @pl.loop(1, chips)
    def _(d):
        hop_copy(lax.rem(chip + d, chips), chip).start()

    kv_sent = []
    for d in range(1, n_c):
        for which in range(2):
            copy = kv_copy(which, d)
            copy.start()
            kv_sent.append(copy)
    for i in range(AHEAD):
        directs(i)
    for s in range(nq):
        to_partner(0, s)

    locals_in[0].wait()
    for j in range(n_f):
        tok_copy(j).wait()
    start_moves()
    for s in range(nq):
        for h in range(HALVES):
            arrived(0, 1, s, h)

        @pl.loop(0, 2)
        def _(j):
            q_part(j, s)

    for copy in locals_in[1:]:
        copy.wait()

    lag = levels - 1
    total = len(stream)
    done = {}
    for step in range(total + lag):
        pass_level(step, 1)
        if step + AHEAD < total:
            directs(step + AHEAD)
        i = step - lag
        for lev in range(2, levels):
            pass_level(step - lev + 1, lev)
        for s in range(nq):
            if s in done and done[s] < n_c:
                if i == nq:
                    while done[s] < n_c:
                        ctx_pass(s, done[s])
                        done[s] += 1
                else:
                    ctx_pass(s, done[s])
                    done[s] += 1
        if i == nq:
            for q in range(chips):
                for plane in range(n_c):
                    ctx_perm[q, :, plane * part:(plane + 1) * part] = ctx_all[
                        plane, :, q * part:(q + 1) * part
                    ]
        if i >= 0:
            if levels > 1:
                compute_early(i)
                pass_level(i, levels)
            if i == 0:
                for copy in kv_sent:
                    copy.wait_recv()
            compute(i)
            if stream[i][0] == 0:
                done[stream[i][1]] = 1
            if i == nq - 1:
                acc[...] = jnp.zeros_like(acc)
                ctx_pass(nq - 1, 1)
                done[nq - 1] = 2
        if step + 1 + AHEAD == max(nq, AHEAD + 1):
            wait_moves()
            for s in range(nw):
                to_partner(1, s)

    assert len(sent) == send_sem.shape[0]
    for copy in sent + kv_sent:
        copy.wait_send()
    for s in range(nq):
        ctx_drain(s)

    @pl.loop(0, chips)
    def _(q):
        @pl.when(q != chip)
        def _():
            hop_copy(q, chip).wait_send()

        home, _ = owner(q)

        @pl.when(home != c)
        def _():
            move(piece(chip), q).wait_send()

    for s in range(nw):
        for k in range(2):
            out_copy(s, k).wait()


def body(n_f, n_c, tokens, wq, wo, key_cache, value_cache, key_blocks):
    rows, width = tokens.shape
    depth = width // n_f
    qcols = wq.shape[1]
    cache = key_cache.shape[0]
    blk_dev = cache // BLOCK
    kv_cols = key_cache.shape[1] // n_c
    n_list = key_blocks.shape[2]
    cosine, sine = tables(rows, cache * n_c)
    nq = max(1, min(4, qcols // HEAD))
    ratio = n_f // n_c
    chips = n_f // 2
    part = wo.shape[0] // chips
    moved = (part * n_c, wo.shape[1] * ratio // 2)
    nw = max(1, min(4, moved[1] // LANES))
    any_spec = pl.BlockSpec(memory_space=pl.ANY)
    bf16 = jnp.bfloat16
    f32 = jnp.float32
    dma = pltpu.SemaphoreType.DMA
    return pl.pallas_call(
        functools.partial(kernel, (n_f, n_c, nq, nw)),
        out_shape=jax.ShapeDtypeStruct((rows, width // n_c), bf16),
        in_specs=[pl.BlockSpec(memory_space=pltpu.SMEM)] + [any_spec] * 7,
        out_specs=any_spec,
        scratch_shapes=[
            pltpu.VMEM((n_f, rows, depth), bf16),
            pltpu.VMEM((n_f,) + wq.shape, bf16),
            pltpu.VMEM((n_f,) + moved, bf16),
            pltpu.VMEM((blk_dev * n_c, BLOCK, kv_cols), bf16),
            pltpu.VMEM((blk_dev * n_c, BLOCK, kv_cols), bf16),
            pltpu.VMEM((rows, max(qcols, width // n_c)), f32),
            pltpu.VMEM((rows, qcols), bf16),
            pltpu.VMEM((n_list * BLOCK, HEAD), bf16),
            pltpu.VMEM((n_list * BLOCK, HEAD), bf16),
            pltpu.VMEM((BLOCK, n_list * BLOCK), f32),
            pltpu.VMEM((n_c, rows, qcols), bf16),
            pltpu.VMEM((chips, rows, n_c * part), bf16),
            pltpu.VMEM((rows, width // n_c), bf16),
            pltpu.VMEM((chips, part, wo.shape[1]), bf16),
            pltpu.VMEM((rows, HEAD), f32),
            pltpu.VMEM((rows, HEAD), f32),
            dma((n_f,)),
            dma((5,)),
            dma(((nq + nw) * HALVES * (n_f - 1),)),
            dma((n_f, nq, HALVES)),
            dma((n_f, nw, HALVES)),
            dma((2, n_c)),
            dma((2, n_c)),
            dma((nq, n_c, 2)),
            dma((nq, n_c)),
            dma((chips,)),
            dma((ratio // 2, n_c)),
            dma((ratio // 2,)),
            dma((chips,)),
            dma((chips,)),
            dma((nw, 2)),
        ],
        compiler_params=pltpu.CompilerParams(
            collective_id=0, has_side_effects=True, vmem_limit_bytes=67043328
        ),
    )(
        key_blocks,
        tokens,
        wq,
        wo,
        key_cache.reshape(blk_dev, BLOCK, key_cache.shape[1]),
        value_cache.reshape(blk_dev, BLOCK, value_cache.shape[1]),
        jnp.asarray(cosine, jnp.float32),
        jnp.asarray(sine, jnp.float32),
    )


def solution(mesh):
    in_specs = (
        P("fsdp", None),
        P("fsdp", "ctx"),
        P("ctx", "fsdp"),
        P(("fsdp", "ctx"), None),
        P(("fsdp", "ctx"), None),
        P("fsdp", None, None),
    )
    step = functools.partial(body, mesh.shape["fsdp"], mesh.shape["ctx"])
    return jax.shard_map(
        step, mesh=mesh, in_specs=in_specs, out_specs=P("fsdp", "ctx"), check_vma=False
    )
```

time: 252 us -> 175 us (0.69)
  the two profiles are of different devices: /device:TPU:29 before, /device:TPU:0 now
where the time goes in v1:
time: 175 us
  Pallas kernels  171 us (98%)
  local copies, waits for them, and re-layouts  3.16 us (2%)
    pallas_call x1, Pallas kernels, body(): pl.pallas_call(functools.partial(kernel, (n_f, n_c, nq, nw)), out_shape=j...  171 us

profile of v1, /device:TPU:0, one launch (start us, length us, event | category | flops | bytes accessed | tf_op | source)
XLA Modules:
  0.0 174.6 jit_solution(5505472473633273)
XLA Ops:
  0.0 171.5 %shard_map.82 = bf16[512,2048]{1,0:T(8,128)(2,1)} custom-call(s32[1,4,8]{2,1,0:T(4,128)} %lists.1, bf16[512,8192]{1,0:T(8,128)(2,1)} %tokens.1, bf16[1024,1024]{1,0:T(8,128)(2,1)} %wq.1, bf16[1024,1024]{1,0:T(8,128)(2,1)} %wo.1, bf16[2,128,1024]{2,1,0:T(8,128)(2,1)} %bitcast.2, bf16[2,128,1024]{2,1,0:T(8,128)(2,1)} %bitcast.3, ...), custom_call_target="tpu_custom_call" | custom-call | tf_op jit(solution)/shard_map/pallas_call | solution.py:543
  171.5 3.2 %copy.10 = bf16[512,2048]{1,0:T(8,128)(2,1)} copy(bf16[512,2048]{1,0:T(8,128)(2,1)} %shard_map.82) | data formatting | bytes 4194304

commit v2 on v1

--- a/solution.py
+++ b/solution.py
@@ -47,10 +47,11 @@
     lists, tokens, wq, wo, kc, vc, cos_in, sin_in,
     out,
     tok, wq_buf, wo_buf, k_buf, v_buf, acc, qc, k_pick, v_pick, bias, ctx_all, ctx_perm, staged, hop, cos_ref, sin_ref,
+    rs_buf, rs_sum, rs_recv,
     tok_sem, own_sem, send_sem, wq_sem, wo_sem, kv_send, kv_sem, ctx_send, ctx_sem,
-    move_send, move_sem, keep_sem, hop_send, hop_sem, out_sem,
+    move_send, move_sem, keep_sem, hop_send, hop_sem, out_sem, rs_sem, give_send, give_sem,
 ):
-    n_f, n_c, nq, nw = cfg
+    n_f, n_c, nq, nw, rs_cols = cfg
     chips = n_f // 2
     bits = [1 << i for i in range(chips.bit_length() - 1)]
     levels = len(bits)
@@ -64,6 +65,8 @@
     qp = qcols // nq
     qh = wq_buf.shape[1] // HALVES
     wo_cols = wo.shape[1]
+    t_cols = wo_cols - rs_cols
+    rh = wo.shape[0] // HALVES
     wp = wo_buf.shape[2] // nw
     wh = wo_buf.shape[1] // HALVES
     part = wo.shape[0] // chips
@@ -90,12 +93,15 @@
     def view(kind, ref, s, h):
         if kind == 0:
             return ref.at[pl.ds(h * qh, qh), pl.ds(s * qp, qp)]
+        if kind == 2:
+            return ref.at[pl.ds(h * rh, rh), pl.ds(0, rs_cols)]
         return ref.at[pl.ds(h * wh, wh), pl.ds(s * wp, wp)]
 
-    shard = (wq, wo_buf.at[0])
-    bufs = (wq_buf, wo_buf)
-    sems = (wq_sem, wo_sem)
-    stream = [(0, s) for s in range(nq)] + [(1, s) for s in range(nw)]
+    shard = (wq, wo_buf.at[0], wo)
+    bufs = (wq_buf, wo_buf, rs_buf)
+    sems = (wq_sem, wo_sem, rs_sem)
+    stream = [(0, s) for s in range(nq)] + ([(2, 0)] if rs_cols else []) + [(1, s) for s in range(nw)]
+    first_wo = stream.index((1, 0))
 
     def send(kind, src, slot, s, h, to):
         copy = pltpu.make_async_remote_copy(
@@ -161,7 +167,7 @@
     chip = lax.div(f, 2)
 
     def piece(q):
-        return wo.at[pl.ds(pl.multiple_of(q * part, part), part), :]
+        return wo.at[pl.ds(pl.multiple_of(q * part, part), part), pl.ds(rs_cols, t_cols)]
 
     def hop_copy(q, source):
         return pltpu.make_async_remote_copy(
@@ -177,7 +183,7 @@
         return wo_buf.at[
             0,
             pl.ds(pl.multiple_of(plane * part, part), part),
-            pl.ds(pl.multiple_of(i * wo_cols, wo_cols), wo_cols),
+            pl.ds(pl.multiple_of(i * t_cols, t_cols), t_cols),
         ]
 
     def owner(p):
@@ -343,17 +349,109 @@
 
     def share(j, s):
         target = flip(j)
-        i, offset = divmod(s * wp, wo_cols)
-        start = pl.multiple_of((2 * i + lax.rem(target, 2)) * wo_cols + offset, LANES)
+        i, offset = divmod(s * wp, t_cols)
+        start = pl.multiple_of((2 * i + lax.rem(target, 2)) * wo_cols + rs_cols + offset, LANES)
         acc[:, pl.ds(start, wp)] += jnp.dot(
             ctx_perm[lax.div(target, 2)], wo_buf[j, :, s * wp:(s + 1) * wp],
             preferred_element_type=jnp.float32,
         )
 
+    def out_cols(s, k):
+        if s == nw:
+            return pl.ds(k * wo_cols, rs_cols)
+        i, offset = divmod(s * wp, t_cols)
+        return pl.ds((2 * i + k) * wo_cols + rs_cols + offset, wp)
+
     def out_copy(s, k):
-        i, offset = divmod(s * wp, wo_cols)
-        cols = pl.ds((2 * i + k) * wo_cols + offset, wp)
+        cols = out_cols(s, k)
         return pltpu.make_async_copy(staged.at[:, cols], out.at[:, cols], out_sem.at[s, k])
+
+    def gift(home, k):
+        return tok.at[home, :, pl.ds(k * rs_cols, rs_cols)]
+
+    def give(home, k, side):
+        slot = jnp.where(home == c + 2 * side - 1, n_c * (1 - side) + home * side, home)
+        return pltpu.make_async_remote_copy(
+            src_ref=gift(home, k),
+            dst_ref=rs_recv.at[slot, k],
+            send_sem=give_send.at[home, k],
+            recv_sem=give_sem.at[slot, k],
+            device_id=(f, c + 2 * side - 1),
+            device_id_type=MESH,
+        )
+
+    def got(slot, k):
+        pltpu.make_async_remote_copy(
+            src_ref=rs_recv.at[slot, k],
+            dst_ref=rs_recv.at[slot, k],
+            send_sem=give_send.at[0, k],
+            recv_sem=give_sem.at[slot, k],
+            device_id=peer(1),
+            device_id_type=MESH,
+        ).wait_recv()
+
+    def rs_start():
+        locals_in[5].wait()
+
+        @pl.loop(0, n_f)
+        def _(j):
+            @pl.when(lax.rem(j, 2) == 1)
+            def _():
+                for h in range(HALVES):
+                    arrived(2, j, 0, h)
+
+            target = flip(j)
+            cols = pl.ds(pl.multiple_of(lax.rem(target, 2) * rs_cols, LANES), rs_cols)
+            tok[lax.div(target, 2), :, cols] = jnp.dot(
+                qc[...], rs_buf[j], preferred_element_type=jnp.float32
+            ).astype(jnp.bfloat16)
+
+        @pl.when(c == 0)
+        def _():
+            for home in range(n_c - 1, 0, -1):
+                for k in range(2):
+                    give(home, k, 1).start()
+
+        @pl.when(c == n_c - 1)
+        def _():
+            for home in range(n_c - 1):
+                for k in range(2):
+                    give(home, k, 0).start()
+
+    def rs_pass(e, k):
+        def add(home, side):
+            got(home, k)
+            cols = slice(k * rs_cols, (k + 1) * rs_cols)
+            tok[home, :, cols] = (
+                tok[home, :, cols].astype(jnp.float32) + rs_recv[home, k].astype(jnp.float32)
+            ).astype(jnp.bfloat16)
+            give(home, k, side).start()
+
+        @pl.when(jnp.logical_and(c > 0, c + e < n_c))
+        def _():
+            add(c + e, 1)
+
+        @pl.when(jnp.logical_and(c < n_c - 1, c - e >= 0))
+        def _():
+            add(c - e, 0)
+
+    def take():
+        for k in range(2):
+            cols = slice(k * rs_cols, (k + 1) * rs_cols)
+            rs_sum[...] = tok[c, :, cols].astype(jnp.float32)
+
+            @pl.when(c > 0)
+            def _():
+                got(c, k)
+                rs_sum[...] += rs_recv[c, k].astype(jnp.float32)
+
+            @pl.when(c < n_c - 1)
+            def _():
+                got(n_c, k)
+                rs_sum[...] += rs_recv[n_c, k].astype(jnp.float32)
+
+            staged[:, out_cols(nw, k)] = rs_sum[...].astype(jnp.bfloat16)
+            out_copy(nw, k).start()
 
     last_slot = 2 * min(m for m in masks if level[m] == levels)
 
@@ -391,8 +489,7 @@
             return
         shares(s, (last_slot if levels == 2 else 4) if levels > 1 else 0, n_f)
         for k in range(2):
-            p, offset = divmod(s * wp, wo_cols)
-            cols = pl.ds((2 * p + k) * wo_cols + offset, wp)
+            cols = out_cols(s, k)
             staged[:, cols] = acc[:, cols].astype(jnp.bfloat16)
             out_copy(s, k).start()
 
@@ -408,6 +505,8 @@
         pltpu.make_async_copy(cos_in, cos_ref, own_sem.at[3]),
         pltpu.make_async_copy(sin_in, sin_ref, own_sem.at[4]),
     ]
+    if rs_cols:
+        locals_in.append(pltpu.make_async_copy(wo.at[:, pl.ds(0, rs_cols)], rs_buf.at[0], own_sem.at[5]))
 
     barrier = pltpu.get_barrier_semaphore()
     signalled = 0
@@ -438,6 +537,8 @@
         directs(i)
     for s in range(nq):
         to_partner(0, s)
+    if rs_cols:
+        to_partner(2, 0)
 
     locals_in[0].wait()
     for j in range(n_f):
@@ -451,37 +552,49 @@
         def _(j):
             q_part(j, s)
 
-    for copy in locals_in[1:]:
+    for copy in locals_in[1:5]:
         copy.wait()
 
     lag = levels - 1
     total = len(stream)
     done = {}
+    queued = AHEAD
+
+    def ctx_next(s):
+        if done[s] < n_c:
+            ctx_pass(s, done[s])
+            done[s] += 1
+
     for step in range(total + lag):
         pass_level(step, 1)
-        if step + AHEAD < total:
-            directs(step + AHEAD)
         i = step - lag
+        while queued < total and queued <= step + AHEAD and not (rs_cols and step == nq - 1 and queued > nq):
+            directs(queued)
+            queued += 1
         for lev in range(2, levels):
             pass_level(step - lev + 1, lev)
         for s in range(nq):
-            if s in done and done[s] < n_c:
-                if i == nq:
-                    while done[s] < n_c:
-                        ctx_pass(s, done[s])
-                        done[s] += 1
-                else:
-                    ctx_pass(s, done[s])
-                    done[s] += 1
-        if i == nq:
+            if s in done and not (rs_cols and s == nq - 1):
+                ctx_next(s)
+        if rs_cols and step == nq + 1:
+            for k in range(2):
+                for e in range(n_c - 2, 1, -1):
+                    rs_pass(e, k)
+                ctx_next(nq - 1)
+        if i == first_wo:
+            for s in range(nq):
+                while done[s] < n_c:
+                    ctx_next(s)
             for q in range(chips):
                 for plane in range(n_c):
                     ctx_perm[q, :, plane * part:(plane + 1) * part] = ctx_all[
                         plane, :, q * part:(q + 1) * part
                     ]
-        if i >= 0:
+        if i >= 0 and stream[i][0] != 2:
             if levels > 1:
                 compute_early(i)
+                if rs_cols and step == total + lag - 1:
+                    take()
                 pass_level(i, levels)
             if i == 0:
                 for copy in kv_sent:
@@ -490,10 +603,15 @@
             if stream[i][0] == 0:
                 done[stream[i][1]] = 1
             if i == nq - 1:
+                if rs_cols:
+                    pass_level(nq, 2)
+                    rs_start()
                 acc[...] = jnp.zeros_like(acc)
-                ctx_pass(nq - 1, 1)
-                done[nq - 1] = 2
-        if step + 1 + AHEAD == max(nq, AHEAD + 1):
+                ctx_next(nq - 1)
+            if rs_cols and i == first_wo:
+                for k in range(2):
+                    rs_pass(1, k)
+        if step + 1 + AHEAD == max(first_wo, AHEAD + 1):
             wait_moves()
             for s in range(nw):
                 to_partner(1, s)
@@ -516,7 +634,14 @@
         def _():
             move(piece(chip), q).wait_send()
 
-    for s in range(nw):
+    if rs_cols:
+        for k in range(2):
+            @pl.loop(0, n_c)
+            def _(home):
+                @pl.when(home != c)
+                def _():
+                    give(home, k, jnp.where(home > c, 1, 0)).wait_send()
+    for s in range(nw + (1 if rs_cols else 0)):
         for k in range(2):
             out_copy(s, k).wait()
 
@@ -534,14 +659,18 @@
     ratio = n_f // n_c
     chips = n_f // 2
     part = wo.shape[0] // chips
-    moved = (part * n_c, wo.shape[1] * ratio // 2)
-    nw = max(1, min(4, moved[1] // LANES))
+    rs_cols = wo.shape[1] // 4 if ratio == 2 and n_f == chips * 2 == n_c * 2 and chips.bit_length() == 3 and wo.shape[1] % (4 * LANES) == 0 else 0
+    t_cols = wo.shape[1] - rs_cols
+    moved = (part * n_c, t_cols * ratio // 2)
+    nw = moved[1] // rs_cols if rs_cols else max(1, min(4, moved[1] // LANES))
+    rs_shape = (wo.shape[0], rs_cols) if rs_cols else (16, LANES)
+    share_shape = (n_c + 1, 2, rows, rs_cols) if rs_cols else (1, 1, 16, LANES)
     any_spec = pl.BlockSpec(memory_space=pl.ANY)
     bf16 = jnp.bfloat16
     f32 = jnp.float32
     dma = pltpu.SemaphoreType.DMA
     return pl.pallas_call(
-        functools.partial(kernel, (n_f, n_c, nq, nw)),
+        functools.partial(kernel, (n_f, n_c, nq, nw, rs_cols)),
         out_shape=jax.ShapeDtypeStruct((rows, width // n_c), bf16),
         in_specs=[pl.BlockSpec(memory_space=pltpu.SMEM)] + [any_spec] * 7,
         out_specs=any_spec,
@@ -559,12 +688,15 @@
             pltpu.VMEM((n_c, rows, qcols), bf16),
             pltpu.VMEM((chips, rows, n_c * part), bf16),
             pltpu.VMEM((rows, width // n_c), bf16),
-            pltpu.VMEM((chips, part, wo.shape[1]), bf16),
+            pltpu.VMEM((chips, part, t_cols), bf16),
             pltpu.VMEM((rows, HEAD), f32),
             pltpu.VMEM((rows, HEAD), f32),
+            pltpu.VMEM((n_f if rs_cols else 1,) + rs_shape, bf16),
+            pltpu.VMEM(share_shape[2:], f32),
+            pltpu.VMEM(share_shape, bf16),
             dma((n_f,)),
-            dma((5,)),
-            dma(((nq + nw) * HALVES * (n_f - 1),)),
+            dma((6,)),
+            dma(((nq + nw + (1 if rs_cols else 0)) * HALVES * (n_f - 1),)),
             dma((n_f, nq, HALVES)),
             dma((n_f, nw, HALVES)),
             dma((2, n_c)),
@@ -576,7 +708,10 @@
             dma((ratio // 2,)),
             dma((chips,)),
             dma((chips,)),
-            dma((nw, 2)),
+            dma((nw + 1, 2)),
+            dma((n_f, 1, HALVES)),
+            dma((n_c, 2)),
+            dma((n_c + 1, 2)),
         ],
         compiler_params=pltpu.CompilerParams(
             collective_id=0, has_side_effects=True, vmem_limit_bytes=67043328

time: 175 us -> 170 us (0.971)
  Pallas kernels: 171 us -> 166 us
    pallas_call x1, Pallas kernels: 171 us -> 166 us  [body(): pl.pallas_call(functools.partial(kernel, (n_f, n_c, nq, nw, rs_cols)), ou...]
where the time goes in v2:
time: 170 us
  Pallas kernels  166 us (98%)
  local copies, waits for them, and re-layouts  3.16 us (2%)
    pallas_call x1, Pallas kernels, body(): pl.pallas_call(functools.partial(kernel, (n_f, n_c, nq, nw, rs_cols)), ou...  166 us

profile of v2, /device:TPU:0, one launch (start us, length us, event | category | flops | bytes accessed | tf_op | source)
XLA Modules:
  0.0 169.6 jit_solution(16890753455505647043)
XLA Ops:
  0.0 166.4 %shard_map.82 = bf16[512,2048]{1,0:T(8,128)(2,1)} custom-call(s32[1,4,8]{2,1,0:T(4,128)} %lists.1, bf16[512,8192]{1,0:T(8,128)(2,1)} %tokens.1, bf16[1024,1024]{1,0:T(8,128)(2,1)} %wq.1, bf16[1024,1024]{1,0:T(8,128)(2,1)} %wo.1, bf16[2,128,1024]{2,1,0:T(8,128)(2,1)} %bitcast.2, bf16[2,128,1024]{2,1,0:T(8,128)(2,1)} %bitcast.3, ...), custom_call_target="tpu_custom_call" | custom-call | tf_op jit(solution)/shard_map/pallas_call | solution.py:672
  166.4 3.2 %copy.10 = bf16[512,2048]{1,0:T(8,128)(2,1)} copy(bf16[512,2048]{1,0:T(8,128)(2,1)} %shard_map.82) | data formatting | bytes 4194304

commit v3 on v2

--- a/solution.py
+++ b/solution.py
@@ -46,12 +46,13 @@
     cfg,
     lists, tokens, wq, wo, kc, vc, cos_in, sin_in,
     out,
-    tok, wq_buf, wo_buf, k_buf, v_buf, acc, qc, k_pick, v_pick, bias, ctx_all, ctx_perm, staged, hop, cos_ref, sin_ref,
-    rs_buf, rs_sum, rs_recv,
+    tok, wq_buf, wo_buf, k_buf, v_buf, acc, qc, k_pick, v_pick, bias, ctx_all, ctx_perm, hop, cos_ref, sin_ref,
+    rs_buf, rs_recv,
     tok_sem, own_sem, send_sem, wq_sem, wo_sem, kv_send, kv_sem, ctx_send, ctx_sem,
-    move_send, move_sem, keep_sem, hop_send, hop_sem, out_sem, rs_sem, give_send, give_sem,
+    move_send, move_sem, keep_sem, hop_send, hop_sem, round_sem, rs_sem, give_send, give_sem,
 ):
-    n_f, n_c, nq, nw, rs_cols = cfg
+    n_f, n_c, nq, cuts, rs_cols = cfg
+    nw = len(cuts)
     chips = n_f // 2
     bits = [1 << i for i in range(chips.bit_length() - 1)]
     levels = len(bits)
@@ -67,7 +68,6 @@
     wo_cols = wo.shape[1]
     t_cols = wo_cols - rs_cols
     rh = wo.shape[0] // HALVES
-    wp = wo_buf.shape[2] // nw
     wh = wo_buf.shape[1] // HALVES
     part = wo.shape[0] // chips
     ratio = n_f // n_c
@@ -95,7 +95,7 @@
             return ref.at[pl.ds(h * qh, qh), pl.ds(s * qp, qp)]
         if kind == 2:
             return ref.at[pl.ds(h * rh, rh), pl.ds(0, rs_cols)]
-        return ref.at[pl.ds(h * wh, wh), pl.ds(s * wp, wp)]
+        return ref.at[pl.ds(h * wh, wh), pl.ds(*cuts[s])]
 
     shard = (wq, wo_buf.at[0], wo)
     bufs = (wq_buf, wo_buf, rs_buf)
@@ -158,10 +158,22 @@
             src_ref=src.at[:, :, pl.ds(pl.multiple_of(other * kv_cols, LANES), kv_cols)],
             dst_ref=dst.at[pl.ds(c * blk_dev, blk_dev)],
             send_sem=kv_send.at[which, d],
-            recv_sem=kv_sem.at[which, d],
+            recv_sem=kv_sem.at[which, c],
             device_id=(f, other),
             device_id_type=MESH,
         )
+
+    def kv_wait(which, d):
+        plane = lax.rem(c + d, n_c)
+        dst = (k_buf, v_buf)[which].at[pl.ds(plane * blk_dev, blk_dev)]
+        pltpu.make_async_remote_copy(
+            src_ref=dst,
+            dst_ref=dst,
+            send_sem=kv_send.at[which, d],
+            recv_sem=kv_sem.at[which, plane],
+            device_id=peer(1),
+            device_id_type=MESH,
+        ).wait_recv()
 
     core = lax.rem(f, 2)
     chip = lax.div(f, 2)
@@ -349,22 +361,20 @@
 
     def share(j, s):
         target = flip(j)
-        i, offset = divmod(s * wp, t_cols)
+        first, width = cuts[s]
+        i, offset = divmod(first, t_cols)
         start = pl.multiple_of((2 * i + lax.rem(target, 2)) * wo_cols + rs_cols + offset, LANES)
-        acc[:, pl.ds(start, wp)] += jnp.dot(
-            ctx_perm[lax.div(target, 2)], wo_buf[j, :, s * wp:(s + 1) * wp],
+        acc[:, pl.ds(start, width)] += jnp.dot(
+            ctx_perm[lax.div(target, 2)], wo_buf[j, :, first:first + width],
             preferred_element_type=jnp.float32,
         )
 
     def out_cols(s, k):
         if s == nw:
             return pl.ds(k * wo_cols, rs_cols)
-        i, offset = divmod(s * wp, t_cols)
-        return pl.ds((2 * i + k) * wo_cols + rs_cols + offset, wp)
-
-    def out_copy(s, k):
-        cols = out_cols(s, k)
-        return pltpu.make_async_copy(staged.at[:, cols], out.at[:, cols], out_sem.at[s, k])
+        first, width = cuts[s]
+        i, offset = divmod(first, t_cols)
+        return pl.ds((2 * i + k) * wo_cols + rs_cols + offset, width)
 
     def gift(home, k):
         return tok.at[home, :, pl.ds(k * rs_cols, rs_cols)]
@@ -438,20 +448,20 @@
     def take():
         for k in range(2):
             cols = slice(k * rs_cols, (k + 1) * rs_cols)
-            rs_sum[...] = tok[c, :, cols].astype(jnp.float32)
+            place = out_cols(nw, k)
+            acc[:, place] = tok[c, :, cols].astype(jnp.float32)
 
             @pl.when(c > 0)
             def _():
                 got(c, k)
-                rs_sum[...] += rs_recv[c, k].astype(jnp.float32)
+                acc[:, place] += rs_recv[c, k].astype(jnp.float32)
 
             @pl.when(c < n_c - 1)
             def _():
                 got(n_c, k)
-                rs_sum[...] += rs_recv[n_c, k].astype(jnp.float32)
-
-            staged[:, out_cols(nw, k)] = rs_sum[...].astype(jnp.bfloat16)
-            out_copy(nw, k).start()
+                acc[:, place] += rs_recv[n_c, k].astype(jnp.float32)
+
+            out[:, place] = acc[:, place].astype(jnp.bfloat16)
 
     last_slot = 2 * min(m for m in masks if level[m] == levels)
 
@@ -490,8 +500,7 @@
         shares(s, (last_slot if levels == 2 else 4) if levels > 1 else 0, n_f)
         for k in range(2):
             cols = out_cols(s, k)
-            staged[:, cols] = acc[:, cols].astype(jnp.bfloat16)
-            out_copy(s, k).start()
+            out[:, cols] = acc[:, cols].astype(jnp.bfloat16)
 
     def tok_copy(j):
         start = pl.multiple_of(flip(j) * depth, LANES)
@@ -509,32 +518,58 @@
         locals_in.append(pltpu.make_async_copy(wo.at[:, pl.ds(0, rs_cols)], rs_buf.at[0], own_sem.at[5]))
 
     barrier = pltpu.get_barrier_semaphore()
-    signalled = 0
-    for x in [1] + [2 * m for m in masks]:
-        pl.semaphore_signal(barrier, inc=1, device_id=peer(x), device_id_type=MESH)
-        signalled += 1
-    for d in range(1, n_c):
-        pl.semaphore_signal(barrier, inc=1, device_id=(f, lax.rem(c + d, n_c)), device_id_type=MESH)
-        signalled += 1
+
+    def beside(sem, extra):
+        for b in extra + [2 * b for b in bits]:
+            pl.semaphore_signal(sem, inc=1, device_id=peer(b), device_id_type=MESH)
+
+        @pl.when(c > 0)
+        def _():
+            pl.semaphore_signal(sem, inc=1, device_id=(f, c - 1), device_id_type=MESH)
+
+        @pl.when(c < n_c - 1)
+        def _():
+            pl.semaphore_signal(sem, inc=1, device_id=(f, c + 1), device_id_type=MESH)
+
+    near = len(bits) + jnp.where(c > 0, 1, 0) + jnp.where(c < n_c - 1, 1, 0)
+    beside(barrier, [1])
     for copy in locals_in:
         copy.start()
     for j in range(n_f):
         tok_copy(j).start()
     acc[...] = jnp.zeros_like(acc)
-    pl.semaphore_wait(barrier, signalled)
-
-    @pl.loop(1, chips)
-    def _(d):
-        hop_copy(lax.rem(chip + d, chips), chip).start()
-
-    kv_sent = []
-    for d in range(1, n_c):
-        for which in range(2):
-            copy = kv_copy(which, d)
-            copy.start()
-            kv_sent.append(copy)
-    for i in range(AHEAD):
-        directs(i)
+    pl.semaphore_wait(barrier, near + 1)
+    rounds = max(levels, n_c - 1) - 1
+
+    def kv_start(d):
+        @pl.when(c + d < n_c)
+        def _():
+            for which in range(2):
+                kv_copy(which, d).start()
+
+        @pl.when(c - d >= 0)
+        def _():
+            for which in range(2):
+                kv_copy(which, n_c - d).start()
+
+    def hops(lev):
+        for m in masks:
+            if level[m] == lev:
+                hop_copy(lax.div(flip(2 * m), 2), chip).start()
+
+    beside(round_sem.at[0], [])
+    hops(1)
+    kv_start(1)
+    for r in range(rounds):
+        pl.semaphore_wait(round_sem.at[r], near)
+        if r + 1 < rounds:
+            beside(round_sem.at[r + 1], [])
+        hops(r + 2)
+        if r + 2 < n_c:
+            kv_start(r + 2)
+        if r == 0:
+            for i in range(AHEAD):
+                directs(i)
     for s in range(nq):
         to_partner(0, s)
     if rs_cols:
@@ -597,8 +632,10 @@
                     take()
                 pass_level(i, levels)
             if i == 0:
-                for copy in kv_sent:
-                    copy.wait_recv()
+                @pl.loop(1, n_c)
+                def _(d):
+                    for which in range(2):
+                        kv_wait(which, d)
             compute(i)
             if stream[i][0] == 0:
                 done[stream[i][1]] = 1
@@ -617,8 +654,14 @@
                 to_partner(1, s)
 
     assert len(sent) == send_sem.shape[0]
-    for copy in sent + kv_sent:
+    for copy in sent:
         copy.wait_send()
+
+    @pl.loop(1, n_c)
+    def _(d):
+        for which in range(2):
+            kv_copy(which, d).wait_send()
+
     for s in range(nq):
         ctx_drain(s)
 
@@ -641,9 +684,6 @@
                 @pl.when(home != c)
                 def _():
                     give(home, k, jnp.where(home > c, 1, 0)).wait_send()
-    for s in range(nw + (1 if rs_cols else 0)):
-        for k in range(2):
-            out_copy(s, k).wait()
 
 
 def body(n_f, n_c, tokens, wq, wo, key_cache, value_cache, key_blocks):
@@ -662,7 +702,13 @@
     rs_cols = wo.shape[1] // 4 if ratio == 2 and n_f == chips * 2 == n_c * 2 and chips.bit_length() == 3 and wo.shape[1] % (4 * LANES) == 0 else 0
     t_cols = wo.shape[1] - rs_cols
     moved = (part * n_c, t_cols * ratio // 2)
-    nw = moved[1] // rs_cols if rs_cols else max(1, min(4, moved[1] // LANES))
+    if rs_cols:
+        widths = [rs_cols] * (moved[1] // rs_cols)
+    else:
+        parts = max(1, min(4, moved[1] // LANES))
+        widths = [moved[1] // parts] * parts
+    cuts = tuple((sum(widths[:s]), w) for s, w in enumerate(widths))
+    nw = len(cuts)
     rs_shape = (wo.shape[0], rs_cols) if rs_cols else (16, LANES)
     share_shape = (n_c + 1, 2, rows, rs_cols) if rs_cols else (1, 1, 16, LANES)
     any_spec = pl.BlockSpec(memory_space=pl.ANY)
@@ -670,10 +716,10 @@
     f32 = jnp.float32
     dma = pltpu.SemaphoreType.DMA
     return pl.pallas_call(
-        functools.partial(kernel, (n_f, n_c, nq, nw, rs_cols)),
-        out_shape=jax.ShapeDtypeStruct((rows, width // n_c), bf16),
+        functools.partial(kernel, (n_f, n_c, nq, cuts, rs_cols)),
+        out_shape=pltpu.VMEM((rows, width // n_c), bf16),
         in_specs=[pl.BlockSpec(memory_space=pltpu.SMEM)] + [any_spec] * 7,
-        out_specs=any_spec,
+        out_specs=pl.BlockSpec(memory_space=pltpu.VMEM),
         scratch_shapes=[
             pltpu.VMEM((n_f, rows, depth), bf16),
             pltpu.VMEM((n_f,) + wq.shape, bf16),
@@ -687,12 +733,10 @@
             pltpu.VMEM((BLOCK, n_list * BLOCK), f32),
             pltpu.VMEM((n_c, rows, qcols), bf16),
             pltpu.VMEM((chips, rows, n_c * part), bf16),
-            pltpu.VMEM((rows, width // n_c), bf16),
             pltpu.VMEM((chips, part, t_cols), bf16),
             pltpu.VMEM((rows, HEAD), f32),
             pltpu.VMEM((rows, HEAD), f32),
             pltpu.VMEM((n_f if rs_cols else 1,) + rs_shape, bf16),
-            pltpu.VMEM(share_shape[2:], f32),
             pltpu.VMEM(share_shape, bf16),
             dma((n_f,)),
             dma((6,)),
@@ -708,13 +752,13 @@
             dma((ratio // 2,)),
             dma((chips,)),
             dma((chips,)),
-            dma((nw + 1, 2)),
+            pltpu.SemaphoreType.REGULAR((max(chips.bit_length() - 1, n_c - 1),)),
             dma((n_f, 1, HALVES)),
             dma((n_c, 2)),
             dma((n_c + 1, 2)),
         ],
         compiler_params=pltpu.CompilerParams(
-            collective_id=0, has_side_effects=True, vmem_limit_bytes=67043328
+            collective_id=0, has_side_effects=True, vmem_limit_bytes=67043328 - 2 * rows * width // n_c - 65536
         ),
     )(
         key_blocks,

time: 170 us -> 166 us (0.976)
  Pallas kernels: 166 us -> 164 us
  local copies, waits for them, and re-layouts: 3.16 us -> 1.32 us
    pallas_call x1, Pallas kernels: 166 us -> 164 us  [body(): pl.pallas_call(functools.partial(kernel, (n_f, n_c, nq, cuts, rs_cols)),...]
    unnamed x1, local copies, waits for them, and re-layouts: 3.16 us -> 1.32 us
where the time goes in v3:
time: 166 us; the launch traced here: 165 us
  Pallas kernels  164 us (99%)
    pallas_call x1, Pallas kernels, body(): pl.pallas_call(functools.partial(kernel, (n_f, n_c, nq, cuts, rs_cols)),...  164 us

profile of v3, /device:TPU:0, one launch (start us, length us, event | category | flops | bytes accessed | tf_op | source)
XLA Modules:
  0.0 165.5 jit_solution(12592869054812576578)
XLA Ops:
  0.0 164.1 %shard_map.82 = bf16[512,2048]{1,0:T(8,128)(2,1)S(1)} custom-call(s32[1,4,8]{2,1,0:T(4,128)} %lists.1, bf16[512,8192]{1,0:T(8,128)(2,1)} %tokens.1, bf16[1024,1024]{1,0:T(8,128)(2,1)} %wq.1, bf16[1024,1024]{1,0:T(8,128)(2,1)} %wo.1, bf16[2,128,1024]{2,1,0:T(8,128)(2,1)} %bitcast.2, bf16[2,128,1024]{2,1,0:T(8,128)(2,1)} %bitcast.3, ...), custom_call_target="tpu_custom_call" | custom-call | tf_op jit(solution)/shard_map/pallas_call | solution.py:718
  164.1 1.3 copy.10

commit v4 on v3

--- a/solution.py
+++ b/solution.py
@@ -47,11 +47,12 @@
     lists, tokens, wq, wo, kc, vc, cos_in, sin_in,
     out,
     tok, wq_buf, wo_buf, k_buf, v_buf, acc, qc, k_pick, v_pick, bias, ctx_all, ctx_perm, hop, cos_ref, sin_ref,
-    rs_buf, rs_recv,
+    rs_buf, rs_recv, pair_buf, pair_hop,
     tok_sem, own_sem, send_sem, wq_sem, wo_sem, kv_send, kv_sem, ctx_send, ctx_sem,
     move_send, move_sem, keep_sem, hop_send, hop_sem, round_sem, rs_sem, give_send, give_sem,
+    pair_src_send, pair_src_sem, pair_move_send, pair_move_sem, pair_keep, pair_send, pair_sem, pair_own_send, pair_own_sem,
 ):
-    n_f, n_c, nq, cuts, rs_cols = cfg
+    n_f, n_c, nq, cuts, rs_cols, pair_cols = cfg
     nw = len(cuts)
     chips = n_f // 2
     bits = [1 << i for i in range(chips.bit_length() - 1)]
@@ -66,7 +67,7 @@
     qp = qcols // nq
     qh = wq_buf.shape[1] // HALVES
     wo_cols = wo.shape[1]
-    t_cols = wo_cols - rs_cols
+    t_cols = wo_cols - rs_cols - pair_cols
     rh = wo.shape[0] // HALVES
     wh = wo_buf.shape[1] // HALVES
     part = wo.shape[0] // chips
@@ -101,6 +102,7 @@
     bufs = (wq_buf, wo_buf, rs_buf)
     sems = (wq_sem, wo_sem, rs_sem)
     stream = [(0, s) for s in range(nq)] + ([(2, 0)] if rs_cols else []) + [(1, s) for s in range(nw)]
+    stream += [(3, 0)] if pair_cols else []
     first_wo = stream.index((1, 0))
 
     def send(kind, src, slot, s, h, to):
@@ -128,6 +130,9 @@
     def directs(i):
         if i < len(stream):
             kind, s = stream[i]
+            if kind == 3:
+                pair_exchange()
+                return
             for h in range(HALVES):
                 for b in bits:
                     send(kind, view(kind, shard[kind], s, h), 2 * b, s, h, 2 * b)
@@ -140,6 +145,10 @@
         if not 0 <= i < len(stream):
             return
         kind, s = stream[i]
+        if kind == 3:
+            if lev == 1:
+                pair_arrive()
+            return
         for h in range(HALVES):
             for m in masks:
                 if level[m] != lev:
@@ -370,11 +379,159 @@
         )
 
     def out_cols(s, k):
+        if s > nw:
+            return pl.ds(k * wo_cols + rs_cols + t_cols, pair_cols)
         if s == nw:
             return pl.ds(k * wo_cols, rs_cols)
         first, width = cuts[s]
         i, offset = divmod(first, t_cols)
         return pl.ds((2 * i + k) * wo_cols + rs_cols + offset, width)
+
+    strip = wo.shape[0] // 4
+    y_of = (0, 0, 3, 3)
+    x_of = (1, 2, 1, 2)
+
+    def quarter(q):
+        return wo.at[pl.ds(q * strip, strip), pl.ds(rs_cols + t_cols, pair_cols)]
+
+    def pair_source(index, src, m, which, to):
+        return pltpu.make_async_remote_copy(
+            src_ref=src,
+            dst_ref=pair_hop.at[m - 1, which],
+            send_sem=pair_src_send.at[index],
+            recv_sem=pair_src_sem.at[m - 1, which],
+            device_id=peer(to),
+            device_id_type=MESH,
+        )
+
+    def pair_sources():
+        return [
+            pair_source(0, quarter(2), 1, 1, 2),
+            pair_source(1, quarter(3), 2, 0, 4),
+            pair_source(2, quarter(0), 1, 0, 2),
+            pair_source(3, quarter(1), 2, 1, 4),
+            pair_source(4, pair_hop.at[0, 1], 3, 1, 4),
+            pair_source(5, pair_hop.at[1, 0], 3, 0, 2),
+        ]
+
+    def pair_move(m, which):
+        home = lax.div(flip(2 * m), 2)
+        q = (y_of, x_of)[which][m]
+        src = quarter(q) if m == 0 else pair_hop.at[m - 1, which]
+        dst = pair_buf.at[0, q, pl.ds(pl.multiple_of(c * strip, strip), strip), :]
+        stay = pltpu.make_async_copy(src, dst, pair_keep.at[which])
+        go = pltpu.make_async_remote_copy(
+            src_ref=src,
+            dst_ref=dst,
+            send_sem=pair_move_send.at[m, which],
+            recv_sem=pair_move_sem.at[which, c],
+            device_id=(f, home),
+            device_id_type=MESH,
+        )
+        return home, stay, go
+
+    def pair_moves(m):
+        for which in range(2):
+            home, stay, go = pair_move(m, which)
+
+            @pl.when(home == c)
+            def _():
+                stay.start()
+
+            @pl.when(home != c)
+            def _():
+                go.start()
+
+    def pair_forward():
+        sources = pair_sources()
+        sources[0].wait_recv()
+        sources[4].start()
+        sources[1].wait_recv()
+        sources[5].start()
+
+    def pair_rest():
+        sources = pair_sources()
+        pair_moves(0)
+        sources[2].wait_recv()
+        pair_moves(1)
+        sources[3].wait_recv()
+        pair_moves(2)
+
+    def pair_far():
+        sources = pair_sources()
+        sources[4].wait_recv()
+        sources[5].wait_recv()
+        pair_moves(3)
+
+    def held(which):
+        side = lax.rem(lax.rem(chip, 2) + lax.rem(c, 2), 2)
+        if which == 1:
+            return side + 1
+        return lax.rem(lax.div(chip, 2) + lax.div(c, 2), 2) * 3
+
+    def pair_swap(which):
+        q = held(which)
+        return pltpu.make_async_remote_copy(
+            src_ref=pair_buf.at[0, q],
+            dst_ref=pair_buf.at[0, q],
+            send_sem=pair_send.at[which],
+            recv_sem=pair_sem.at[which],
+            device_id=peer(4 if which == 0 else 2),
+            device_id_type=MESH,
+        )
+
+    def pair_share(which, fresh):
+        q = 3 - held(which) if fresh else held(which)
+        return pltpu.make_async_remote_copy(
+            src_ref=pair_buf.at[0, q],
+            dst_ref=pair_buf.at[1, q],
+            send_sem=pair_own_send.at[fresh, which],
+            recv_sem=pair_own_sem.at[fresh, which],
+            device_id=peer(1),
+            device_id_type=MESH,
+        )
+
+    def pair_exchange():
+        for which in range(2):
+            q = held(which)
+            here = pair_buf.at[0, q, pl.ds(pl.multiple_of(c * strip, strip), strip), :]
+            pltpu.make_async_copy(here, here, pair_keep.at[which]).wait()
+
+            @pl.loop(1, n_c)
+            def _(d):
+                plane = lax.rem(c + d, n_c)
+                there = pair_buf.at[0, q, pl.ds(pl.multiple_of(plane * strip, strip), strip), :]
+                pltpu.make_async_remote_copy(
+                    src_ref=there,
+                    dst_ref=there,
+                    send_sem=pair_move_send.at[0, which],
+                    recv_sem=pair_move_sem.at[which, plane],
+                    device_id=peer(1),
+                    device_id_type=MESH,
+                ).wait_recv()
+
+            pair_swap(which).start()
+            pair_share(which, 0).start()
+
+    def pair_arrive():
+        for which in range(2):
+            pair_swap(which).wait_recv()
+            pair_share(which, 1).start()
+
+    def pair_compute():
+        for par in range(2):
+            if par == 1:
+                for fresh in range(2):
+                    for which in range(2):
+                        pair_share(which, fresh).wait_recv()
+            side = core if par == 0 else 1 - core
+            start = pl.multiple_of(side * wo_cols + rs_cols + t_cols, LANES)
+
+            @pl.loop(0, 4)
+            def _(q):
+                acc[:, pl.ds(start, pair_cols)] += jnp.dot(
+                    ctx_perm[q], pair_buf[par, q], preferred_element_type=jnp.float32
+                )
 
     def gift(home, k):
         return tok.at[home, :, pl.ds(k * rs_cols, rs_cols)]
@@ -497,7 +654,11 @@
             attend(s)
             ctx_start(s)
             return
-        shares(s, (last_slot if levels == 2 else 4) if levels > 1 else 0, n_f)
+        if kind == 3:
+            pair_compute()
+            s = nw + 1
+        else:
+            shares(s, (last_slot if levels == 2 else 4) if levels > 1 else 0, n_f)
         for k in range(2):
             cols = out_cols(s, k)
             out[:, cols] = acc[:, cols].astype(jnp.bfloat16)
@@ -558,6 +719,9 @@
                 hop_copy(lax.div(flip(2 * m), 2), chip).start()
 
     beside(round_sem.at[0], [])
+    if pair_cols:
+        for copy in pair_sources()[:4]:
+            copy.start()
     hops(1)
     kv_start(1)
     for r in range(rounds):
@@ -567,9 +731,10 @@
         hops(r + 2)
         if r + 2 < n_c:
             kv_start(r + 2)
-        if r == 0:
-            for i in range(AHEAD):
-                directs(i)
+    if pair_cols:
+        pair_forward()
+    for i in range(AHEAD):
+        directs(i)
     for s in range(nq):
         to_partner(0, s)
     if rs_cols:
@@ -579,6 +744,8 @@
     for j in range(n_f):
         tok_copy(j).wait()
     start_moves()
+    if pair_cols:
+        pair_rest()
     for s in range(nq):
         for h in range(HALVES):
             arrived(0, 1, s, h)
@@ -600,8 +767,15 @@
             ctx_pass(s, done[s])
             done[s] += 1
 
-    for step in range(total + lag):
+    last = total + lag - 1
+    if pair_cols:
+        last = total - 1
+    for step in range(last + 1):
         pass_level(step, 1)
+        if pair_cols and step == last:
+            compute(step)
+        if pair_cols and step == 0:
+            pair_far()
         i = step - lag
         while queued < total and queued <= step + AHEAD and not (rs_cols and step == nq - 1 and queued > nq):
             directs(queued)
@@ -627,10 +801,11 @@
                     ]
         if i >= 0 and stream[i][0] != 2:
             if levels > 1:
-                compute_early(i)
-                if rs_cols and step == total + lag - 1:
+                if not (pair_cols and step == last):
+                    compute_early(i)
+                pass_level(i, levels)
+                if rs_cols and step == last:
                     take()
-                pass_level(i, levels)
             if i == 0:
                 @pl.loop(1, n_c)
                 def _(d):
@@ -648,6 +823,8 @@
             if rs_cols and i == first_wo:
                 for k in range(2):
                     rs_pass(1, k)
+            if pair_cols and step == last - 1:
+                compute_early(step)
         if step + 1 + AHEAD == max(first_wo, AHEAD + 1):
             wait_moves()
             for s in range(nw):
@@ -677,6 +854,20 @@
         def _():
             move(piece(chip), q).wait_send()
 
+    if pair_cols:
+        for copy in pair_sources():
+            copy.wait_send()
+        for which in range(2):
+            for m in range(4):
+                home, _, go = pair_move(m, which)
+
+                @pl.when(home != c)
+                def _():
+                    go.wait_send()
+
+            pair_swap(which).wait_send()
+            for fresh in range(2):
+                pair_share(which, fresh).wait_send()
     if rs_cols:
         for k in range(2):
             @pl.loop(0, n_c)
@@ -700,7 +891,8 @@
     chips = n_f // 2
     part = wo.shape[0] // chips
     rs_cols = wo.shape[1] // 4 if ratio == 2 and n_f == chips * 2 == n_c * 2 and chips.bit_length() == 3 and wo.shape[1] % (4 * LANES) == 0 else 0
-    t_cols = wo.shape[1] - rs_cols
+    pair_cols = rs_cols
+    t_cols = wo.shape[1] - rs_cols - pair_cols
     moved = (part * n_c, t_cols * ratio // 2)
     if rs_cols:
         widths = [rs_cols] * (moved[1] // rs_cols)
@@ -709,6 +901,9 @@
         widths = [moved[1] // parts] * parts
     cuts = tuple((sum(widths[:s]), w) for s, w in enumerate(widths))
     nw = len(cuts)
+    strip = wo.shape[0] // 4
+    pair_shape = (2, 4, n_c * strip, pair_cols) if pair_cols else (1, 1, 16, LANES)
+    pair_hop_shape = (3, 2, strip, pair_cols) if pair_cols else (1, 1, 16, LANES)
     rs_shape = (wo.shape[0], rs_cols) if rs_cols else (16, LANES)
     share_shape = (n_c + 1, 2, rows, rs_cols) if rs_cols else (1, 1, 16, LANES)
     any_spec = pl.BlockSpec(memory_space=pl.ANY)
@@ -716,7 +911,7 @@
     f32 = jnp.float32
     dma = pltpu.SemaphoreType.DMA
     return pl.pallas_call(
-        functools.partial(kernel, (n_f, n_c, nq, cuts, rs_cols)),
+        functools.partial(kernel, (n_f, n_c, nq, cuts, rs_cols, pair_cols)),
         out_shape=pltpu.VMEM((rows, width // n_c), bf16),
         in_specs=[pl.BlockSpec(memory_space=pltpu.SMEM)] + [any_spec] * 7,
         out_specs=pl.BlockSpec(memory_space=pltpu.VMEM),
@@ -738,6 +933,8 @@
             pltpu.VMEM((rows, HEAD), f32),
             pltpu.VMEM((n_f if rs_cols else 1,) + rs_shape, bf16),
             pltpu.VMEM(share_shape, bf16),
+            pltpu.VMEM(pair_shape, bf16),
+            pltpu.VMEM(pair_hop_shape, bf16),
             dma((n_f,)),
             dma((6,)),
             dma(((nq + nw + (1 if rs_cols else 0)) * HALVES * (n_f - 1),)),
@@ -756,6 +953,15 @@
             dma((n_f, 1, HALVES)),
             dma((n_c, 2)),
             dma((n_c + 1, 2)),
+            dma((6,)),
+            dma((3, 2)),
+            dma((4, 2)),
+            dma((2, n_c)),
+            dma((2,)),
+            dma((2,)),
+            dma((2,)),
+            dma((2, 2)),
+            dma((2, 2)),
         ],
         compiler_params=pltpu.CompilerParams(
             collective_id=0, has_side_effects=True, vmem_limit_bytes=67043328 - 2 * rows * width // n_c - 65536

time: 166 us -> 163 us (0.982)
  Pallas kernels: 164 us -> 162 us
    pallas_call x1, Pallas kernels: 164 us -> 162 us  [body(): pl.pallas_call(functools.partial(kernel, (n_f, n_c, nq, cuts, rs_cols, pa...]
where the time goes in v4:
time: 163 us
  Pallas kernels  162 us (99%)
    pallas_call x1, Pallas kernels, body(): pl.pallas_call(functools.partial(kernel, (n_f, n_c, nq, cuts, rs_cols, pa...  162 us

profile of v4, /device:TPU:0, one launch (start us, length us, event | category | flops | bytes accessed | tf_op | source)
XLA Modules:
  0.0 162.9 jit_solution(14173695083303411206)
XLA Ops:
  0.0 161.6 %shard_map.82 = bf16[512,2048]{1,0:T(8,128)(2,1)S(1)} custom-call(s32[1,4,8]{2,1,0:T(4,128)} %lists.1, bf16[512,8192]{1,0:T(8,128)(2,1)} %tokens.1, bf16[1024,1024]{1,0:T(8,128)(2,1)} %wq.1, bf16[1024,1024]{1,0:T(8,128)(2,1)} %wo.1, bf16[2,128,1024]{2,1,0:T(8,128)(2,1)} %bitcast.2, bf16[2,128,1024]{2,1,0:T(8,128)(2,1)} %bitcast.3, ...), custom_call_target="tpu_custom_call" | custom-call | tf_op jit(solution)/shard_map/pallas_call | solution.py:913
  161.6 1.3 copy.10
